TPU v7x, 32 devices: a whole 2x2x4 slice. The times are simulated.
32 devices in a mesh: inl: 4 (over x, core), xl: 8 (over z, y).
Axes of the slice: x: 2, y: 2, z: 4, core: 2. Of those that a mesh axis runs over, the one named last changes fastest.
Arguments:
- baseline: float32 [16, 128, 1024], P('inl', 'xl'), may hold values from -600 to 600
- monitor: float32 [16, 128, 1024], P('inl', 'xl'), may hold values from -900 to 900
- shift_model: float32 [4, 32, 128], P(None, None, 'xl'), may hold values from -4 to 4
- knot_start: int32 [32, 4], replicated, may hold values from -12 to 13, as said below
- half_width: int32 [8], P('xl'), may hold values from 1 to 3
Outputs:
- shift_obs: float32 [16, 128, 1024], P('inl', 'xl')
- delta: float32 [4, 32, 128], P(None, 'xl', 'inl')
Inputs may be any that keep to these rules, and one draw needn't show every extreme that they name: `knot_start`: basis function k of a window starts at sample k * 8 - 3 * 4 or one later, relative to the window's first sample.
All inputs are finite; a program needn't handle non-finite values.
Results may differ from a plain program's by a relative error of at most 0.00018.
Values sent between devices are 32-bit elements; how exact they have to be, the bound alone decides.
A program may use at most 64 MiB of HBM per device.

v0:
```python
import jax
import jax.numpy as jnp
from jax import lax
from jax.sharding import PartitionSpec as P

LAGS = 15
TWIN = 12
HMAX = 3
WINLEN = 32
KW = 4
KSTEP = 8
EPSILON = 1e-06
SHARPNESS = 6.0
DAMPING = 0.5


def extended(block, sides, width):
    for axis, dim in sides:
        count = lax.axis_size(axis)
        forward = [(i, i + 1) for i in range(count - 1)]
        backward = [(target, source) for source, target in forward]
        low = lax.ppermute(
            lax.slice_in_dim(block, block.shape[dim] - width, None, axis=dim), axis, forward
        )
        high = lax.ppermute(lax.slice_in_dim(block, 0, width, axis=dim), axis, backward)
        block = jnp.concatenate([low, block, high], axis=dim)
    return block


def spline(offset):
    square = offset * offset
    cubed = square * offset
    piece_one = cubed / 6.0
    piece_two = (-3.0 * cubed + 12.0 * square - 12.0 * offset + 4.0) / 6.0
    piece_three = (3.0 * cubed - 24.0 * square + 60.0 * offset - 44.0) / 6.0
    remain = 4.0 - offset
    piece_four = remain * remain * remain / 6.0
    result = jnp.where(offset < 4.0, piece_four, 0.0 * offset)
    result = jnp.where(offset < 3.0, piece_three, result)
    result = jnp.where(offset < 2.0, piece_two, result)
    result = jnp.where(offset < 1.0, piece_one, result)
    return jnp.where(offset < 0.0, 0.0 * offset, result)


def basis_table(knot_start):
    positions = jnp.arange(WINLEN).astype(jnp.float32)
    offset = (positions[None, None, :] - knot_start[:, :, None].astype(jnp.float32)) / KSTEP
    return spline(offset)


def solve_small(matrix, target):
    lower = [[None] * KW for _ in range(KW)]
    for column in range(KW):
        pivot = matrix[column][column]
        for inner in range(column):
            pivot = pivot - lower[column][inner] * lower[column][inner]
        lower[column][column] = jnp.sqrt(pivot)
        for target_row in range(column + 1, KW):
            entry = matrix[target_row][column]
            for inner in range(column):
                entry = entry - lower[target_row][inner] * lower[column][inner]
            lower[target_row][column] = entry / lower[column][column]
    forward = []
    for column in range(KW):
        entry = target[column]
        for inner in range(column):
            entry = entry - lower[column][inner] * forward[inner]
        forward.append(entry / lower[column][column])
    backward = [None] * KW
    for column in range(KW - 1, -1, -1):
        entry = forward[column]
        for inner in range(column + 1, KW):
            entry = entry - lower[inner][column] * backward[inner]
        backward[column] = entry / lower[column][column]
    return jnp.stack(backward)


def box_time(values):
    samples = values.shape[2]
    width = 2 * TWIN + 1
    padded = jnp.pad(values, ((0, 0), (0, 0), (TWIN, TWIN)))
    partial_sums = {1: padded}
    length = 1
    while 2 * length <= width:
        previous = partial_sums[length]
        partial_sums[2 * length] = previous[:, :, :-length] + previous[:, :, length:]
        length = 2 * length
    total = None
    begin = 0
    remain = width
    while remain > 0:
        if length <= remain:
            piece = partial_sums[length][:, :, begin : begin + samples]
            total = piece if total is None else total + piece
            begin = begin + length
            remain = remain - length
        length = length // 2
    return total


def normal_terms(resid_four, conf_four, table):
    row_count = resid_four.shape[0]
    windows = resid_four.shape[2]
    crossl = resid_four.shape[1]
    grad = jnp.einsum(
        "ixwu,wku->ikwx", conf_four * resid_four, table, precision=lax.Precision.HIGHEST
    )
    hess = jnp.einsum(
        "ixwu,wku,wju->ikjwx", conf_four, table, table, precision=lax.Precision.HIGHEST
    )
    return jnp.concatenate([grad, hess.reshape(row_count, KW * KW, windows, crossl)], axis=1)


def per_device(baseline, monitor, shift_model, knot_start, half_width):
    inline_rows = baseline.shape[0]
    slab_width = baseline.shape[1]
    samples = baseline.shape[2]
    paired = extended(jnp.stack([baseline, monitor]), (("xl", 2),), HMAX)
    base_ext = paired[0]
    moni_ext = paired[1]
    half_span = half_width[0]
    lateral = [
        (jnp.abs(offset) <= half_span).astype(jnp.float32) for offset in range(-HMAX, HMAX + 1)
    ]

    def smooth(values):
        timed = box_time(values)
        total = None
        for place, offset in enumerate(range(-HMAX, HMAX + 1)):
            term = lateral[place] * timed[:, HMAX + offset : HMAX + offset + slab_width]
            total = term if total is None else total + term
        return total

    energy_base = smooth(base_ext * base_ext)
    moni_pad = jnp.pad(moni_ext, ((0, 0), (0, 0), (LAGS, LAGS)))
    energy_mon = smooth(moni_pad * moni_pad)

    def one_lag(lag_index, running):
        total_exp, total_shift, total_corr = running
        lagged = lax.dynamic_slice_in_dim(moni_pad, lag_index, samples, 2)
        correlation = smooth(base_ext * lagged)
        energy = lax.dynamic_slice_in_dim(energy_mon, lag_index, samples, 2)
        normed = correlation / jnp.sqrt(energy_base * energy + EPSILON)
        weight_exp = jnp.exp(SHARPNESS * normed)
        lag_value = jnp.asarray(lag_index - LAGS, jnp.int32).astype(jnp.float32)
        return (
            total_exp + weight_exp,
            total_shift + lag_value * weight_exp,
            total_corr + normed * weight_exp,
        )

    first_lag = one_lag(0, (0.0 * energy_base, 0.0 * energy_base, 0.0 * energy_base))
    total_exp, total_shift, total_corr = lax.fori_loop(1, 2 * LAGS + 1, one_lag, first_lag)
    shift_obs = total_shift / total_exp
    confidence = 0.5 + 0.5 * total_corr / total_exp
    table = basis_table(knot_start)
    modelled = jnp.einsum(
        "kwx,wku->xwu", shift_model, table, precision=lax.Precision.HIGHEST
    ).reshape(slab_width, samples)
    resid = shift_obs - modelled[None]
    resid_piece = lax.all_to_all(resid, "xl", split_axis=2, concat_axis=1, tiled=True)
    conf_piece = lax.all_to_all(confidence, "xl", split_axis=2, concat_axis=1, tiled=True)
    row_count = resid_piece.shape[0]
    crossl = resid_piece.shape[1]
    owned = resid_piece.shape[2] // WINLEN
    table_own = lax.dynamic_slice_in_dim(table, lax.axis_index("xl") * owned, owned, 0)
    resid_four = resid_piece.reshape(row_count, crossl, owned, WINLEN)
    conf_four = conf_piece.reshape(row_count, crossl, owned, WINLEN)
    per_row = normal_terms(resid_four, conf_four, table_own)
    normal = jnp.sum(per_row, axis=0)
    summed = lax.psum(normal, "inl")
    share = summed.shape[2] // lax.axis_size("inl")
    summed = lax.dynamic_slice_in_dim(summed, lax.axis_index("inl") * share, share, 2)
    damping = DAMPING * inline_rows * lax.axis_size("inl")
    matrix = [
        [
            summed[KW + KW * first_k + second_k] + (damping if first_k == second_k else 0.0)
            for second_k in range(KW)
        ]
        for first_k in range(KW)
    ]
    target = [summed[first_k] for first_k in range(KW)]
    delta = solve_small(matrix, target)
    return (shift_obs, delta)


def solution(mesh):
    in_specs = (P("inl", "xl", None), P("inl", "xl", None), P(None, None, "xl"), P(), P("xl"))
    out_specs = (P("inl", "xl", None), P(None, "xl", "inl"))
    return jax.shard_map(
        per_device, mesh=mesh, in_specs=in_specs, out_specs=out_specs, check_vma=False
    )
```

profile of v0, /device:TPU:0, one launch (start us, length us, event | category | flops | bytes accessed | tf_op | source)
XLA Modules:
  0.0 127.3 jit_solution(12901075774814896960)
XLA Ops:
  0.6 1.2 pad_maximum_fusion.2
  1.9 1.3 %collective-permute-start.1 = (f32[2,4,3,1024]{3,2,1,0:T(4,128)S(1)}, f32[2,4,3,1024]{3,2,1,0:T(4,128)S(1)}, u32[]{:S(2)}, u32[]{:S(2)}) collective-permute-start(f32[2,4,3,1024]{3,2,1,0:T(4,128)S(1)} %get-tuple-element.489), channel_id=1, source_target_pairs={{1,0},{2,1},{3,2},{4,3},{5,4},{6,5},{7,6},{9,8},{10,9},{11,10},{12... | collective-permute-start | bytes 294920 | tf_op jit(solution)/shard_map/ppermute | solution.py:25
  3.2 5.5 %collective-permute-start = (f32[2,4,3,1024]{3,2,1,0:T(4,128)S(1)}, f32[2,4,3,1024]{3,2,1,0:T(4,128)S(1)}, u32[]{:S(2)}, u32[]{:S(2)}) collective-permute-start(f32[2,4,3,1024]{3,2,1,0:T(4,128)S(1)} %get-tuple-element.488), channel_id=1, source_target_pairs={{0,1},{1,2},{2,3},{3,4},{4,5},{5,6},{6,7},{8,9},{9,10},{10,11},{11... | collective-permute-start | bytes 294920 | tf_op jit(solution)/shard_map/ppermute | solution.py:22
  8.7 0.8 copy.41
  10.3 0.8 convolution_bitcast_fusion
  12.0 1.2 collective-permute-done
  18.0 56.6 %while.21 = (s32[]{:T(128)}, f32[4,16,1024]{2,1,0:T(8,128)S(1)}, f32[4,16,1024]{2,1,0:T(8,128)S(1)}, f32[4,16,1024]{2,1,0:T(8,128)S(1)}, f32[]{:T(128)}, /*index...) while((s32[]{:T(128)}, f32[4,16,1024]{2,1,0:T(8,128)S(1)}, ...), condition=%wide.region_1.2_spmd, body=%wide.region_0.1_spmd.sunk | while | flops 2143487 | bytes 11726543 | solution.py:153
  74.6 1.7 %copy.36 = f32[4,16,1024]{1,0,2:T(4,128)} copy(f32[4,16,1024]{2,1,0:T(8,128)S(1)} %get-tuple-element.429) | data formatting | bytes 524288 | tf_op jit(solution)/shard_map/while | solution.py:153
  76.3 1.7 %copy.37 = f32[4,16,1024]{1,0,2:T(4,128)} copy(f32[4,16,1024]{2,1,0:T(8,128)S(1)} %get-tuple-element.430) | data formatting | bytes 524288 | tf_op jit(solution)/shard_map/while | solution.py:153
  78.1 0.8 copy.39
  78.9 2.3 %reshape.48 = f32[8,1,8192]{2,1,0:T(1,128)} reshape(f32[1024,4,16]{2,1,0:T(4,128)S(1)} %bitcast.52) | data formatting | bytes 524288
  81.2 6.1 %all-to-all-start = ((f32[8,1,8192]{2,1,0:T(1,128)}), f32[8,1,8192]{2,1,0:T(1,128)S(1)}, u32[]{:S(2)}, u32[]{:S(2)}) async-start(f32[8,1,8192]{2,1,0:T(1,128)} %reshape.48), calls=%async_computation | async-start | bytes 524288 | tf_op jit(solution)/shard_map/all_to_all | solution.py:162
  87.3 4.4 %broadcast_subtract_fusion = (f32[4,16,1024]{1,0,2:T(4,128)}, f32[4,16,1024]{1,0,2:T(4,128)S(1)}) fusion(f32[16,1024]{0,1:T(8,128)S(1)} %bitcast.55, f32[4,16,1024]{1,0,2:T(4,128)} %copy.36, f32[4,16,1024]{1,0,2:T(4,128)} %copy.37), kind=kLoop, calls=%fused_computation.31 | loop fusion | flops 131072 | bytes 1114112 | tf_op jit(solution)/shard_map/sub | solution.py:160
  91.7 3.8 %reshape.50 = f32[8,1,8192]{2,1,0:T(1,128)} reshape(f32[1024,4,16]{2,1,0:T(4,128)} %bitcast.51) | data formatting | bytes 524288
  96.1 5.4 %all-to-all-start.1 = ((f32[8,1,8192]{2,1,0:T(1,128)}), f32[8,1,8192]{2,1,0:T(1,128)S(1)}, u32[]{:S(2)}, u32[]{:S(2)}) async-start(f32[8,1,8192]{2,1,0:T(1,128)} %reshape.50), calls=%async_computation.1 | async-start | bytes 524288 | tf_op jit(solution)/shard_map/all_to_all | solution.py:161
  101.7 1.4 %copy.50 = f32[4,16,1024]{2,1,0:T(8,128)} copy(f32[4,16,1024]{1,0,2:T(4,128)S(1)} %get-tuple-element.474) | data formatting | bytes 524288
  103.7 1.3 reduce
  105.0 1.5 %reshape.49 = f32[1024,4,16]{2,1,0:T(4,128)S(1)} reshape(f32[8,8192]{1,0:T(8,128)S(1)} %reduce) | data formatting | bytes 524288
  107.7 1.0 convolution_bitcast_fusion.1
  108.7 1.1 all-to-all-done.1
  109.9 1.3 reduce.1
  111.1 1.5 %reshape.51 = f32[1024,4,16]{2,1,0:T(4,128)S(1)} reshape(f32[8,8192]{1,0:T(8,128)S(1)} %reduce.1) | data formatting | bytes 524288
  114.2 1.6 %convolution_bitcast_fusion.2 = f32[4,4,4,128]{3,1,0,2:T(4,128)S(1)} fusion(f32[4,128,4,32]{3,2,1,0:T(4,128)S(1)} %mul.591, f32[32,4,32]{2,1,0:T(4,128)} %copy-done.2, s32[]{:T(128)S(6)} %select_n.40), kind=kOutput, calls=%fused_computation.28 | convolution fusion | flops 3145728 | bytes 303108 | tf_op jit(solution)/shard_map/ixwu,wku->ikwx/dot_general | solution.py:105
  115.9 10.5 %psum.7 = f32[20,4,128]{2,1,0:T(4,128)S(1)} all-reduce(f32[20,4,128]{2,1,0:T(4,128)S(1)} %copy.49), channel_id=1, replica_groups=mesh['inl'=4,'xl'=8] {'inl'}, use_global_device_ids=true, to_apply=%region_3.4 | all-reduce | flops 10240 | bytes 81920 | tf_op jit(solution)/shard_map/psum | solution.py:171
  (289 shorter events, 65.4 us)
Async XLA Ops:
  0.6 12.6 %copy-start = (f32[4,16,1024]{2,1,0:T(8,128)S(1)}, f32[4,16,1024]{2,1,0:T(8,128)}, u32[]{:S(2)}) copy-start(f32[4,16,1024]{2,1,0:T(8,128)} %param.8) | copy-start | bytes 786436
  0.6 12.6 %copy-start.1 = (f32[4,16,1024]{2,1,0:T(8,128)S(1)}, f32[4,16,1024]{2,1,0:T(8,128)}, u32[]{:S(2)}) copy-start(f32[4,16,1024]{2,1,0:T(8,128)} %param.7) | copy-start | bytes 786436
  1.9 10.1 %collective-permute-start.1 = (f32[2,4,3,1024]{3,2,1,0:T(4,128)S(1)}, f32[2,4,3,1024]{3,2,1,0:T(4,128)S(1)}, u32[]{:S(2)}, u32[]{:S(2)}) collective-permute-start(f32[2,4,3,1024]{3,2,1,0:T(4,128)S(1)} %get-tuple-element.489), channel_id=1, source_target_pairs={{1,0},{2,1},{3,2},{4,3},{5,4},{6,5},{7,6},{9,8},{10,9},{11,10},{12... | collective-permute-start | bytes 294920 | tf_op jit(solution)/shard_map/ppermute | solution.py:25
  3.2 10.0 %collective-permute-start = (f32[2,4,3,1024]{3,2,1,0:T(4,128)S(1)}, f32[2,4,3,1024]{3,2,1,0:T(4,128)S(1)}, u32[]{:S(2)}, u32[]{:S(2)}) collective-permute-start(f32[2,4,3,1024]{3,2,1,0:T(4,128)S(1)} %get-tuple-element.488), channel_id=1, source_target_pairs={{0,1},{1,2},{2,3},{3,4},{4,5},{5,6},{6,7},{8,9},{9,10},{10,11},{11... | collective-permute-start | bytes 294920 | tf_op jit(solution)/shard_map/ppermute | solution.py:22
  81.2 14.9 %all-to-all-start = ((f32[8,1,8192]{2,1,0:T(1,128)}), f32[8,1,8192]{2,1,0:T(1,128)S(1)}, u32[]{:S(2)}, u32[]{:S(2)}) async-start(f32[8,1,8192]{2,1,0:T(1,128)} %reshape.48), calls=%async_computation | async-start | bytes 524288 | tf_op jit(solution)/shard_map/all_to_all | solution.py:162
  96.1 13.8 %all-to-all-start.1 = ((f32[8,1,8192]{2,1,0:T(1,128)}), f32[8,1,8192]{2,1,0:T(1,128)S(1)}, u32[]{:S(2)}, u32[]{:S(2)}) async-start(f32[8,1,8192]{2,1,0:T(1,128)} %reshape.50), calls=%async_computation.1 | async-start | bytes 524288 | tf_op jit(solution)/shard_map/all_to_all | solution.py:161
  101.7 1.5 %copy-start.2 = (f32[32,4,32]{2,1,0:T(4,128)}, f32[32,4,32]{2,1,0:T(4,128)S(1)}, u32[]{:S(2)}) copy-start(f32[32,4,32]{2,1,0:T(4,128)S(1)} %fusion.46) | copy-start | bytes 49156
where the time goes:
time: 128 us; the launch traced here: 127 us
  other arithmetic  63.6 us (50%)
  local copies, waits for them, and re-layouts  24.9 us (19%)
  starting transfers between devices  18.3 us (14%)
  blocking collectives  10.5 us (8%)
  matrix products  3.41 us (3%)
  waiting for transfers between devices  2.93 us (2%)
  loops' own time  2.02 us (2%)
  between operations  1.66 us (1%)
    add x98, other arithmetic, box_time(): previous[:, :, :-length] + previous[:, :, length:]  21.5 us
    add x31, other arithmetic, one_lag(): total_corr + normed * weight_exp  12 us
    unnamed x12, local copies, waits for them, and re-layouts  11.3 us
    psum x1, blocking collectives, per_device(): summed = lax.psum(normal, 'inl')  10.5 us
    add x33, other arithmetic, box_time(): total = piece if total is None else total + piece  9.07 us
    all_to_all x1, starting transfers between devices, per_device(): lax.all_to_all(confidence, 'xl', split_axis=2, concat_axis=1, tiled=True)  6.08 us
    slice x33, local copies, waits for them, and re-layouts, box_time(): previous[:, :, :-length] + previous[:, :, length:]  5.94 us
    ppermute x1, starting transfers between devices, extended(): lax.ppermute(lax.slice_in_dim(block, block.shape[dim] - width, None, axis...  5.51 us
  transfers between devices with their start and end apart: 4, of which 3 were waited for; matrix products, arithmetic and copies ran while one was open for 14% of the time, Pallas kernels for 0%

commit v1 on v0

--- a/solution.py
+++ b/solution.py
@@ -158,7 +158,9 @@
         "kwx,wku->xwu", shift_model, table, precision=lax.Precision.HIGHEST
     ).reshape(slab_width, samples)
     resid = shift_obs - modelled[None]
-    resid_piece = lax.all_to_all(resid, "xl", split_axis=2, concat_axis=1, tiled=True)
+    resid_piece = jnp.concatenate(
+        lax.all_to_all(jnp.stack(jnp.split(resid, lax.axis_size("xl"), axis=2)), "xl", 0, 0), axis=1
+    )
     conf_piece = lax.all_to_all(confidence, "xl", split_axis=2, concat_axis=1, tiled=True)
     row_count = resid_piece.shape[0]
     crossl = resid_piece.shape[1]

time: 128 us -> 125 us (0.977)
  waiting for transfers between devices: 2.93 us -> 14.7 us
  local copies, waits for them, and re-layouts: 24.9 us -> 18.9 us
  other arithmetic: 63.6 us -> 58.7 us
  starting transfers between devices: 18.3 us -> 15.5 us
    all_to_all x1, waiting for transfers between devices: 0.61 us -> 7.35 us  [per_device(): lax.all_to_all(confidence, 'xl', split_axis=2, concat_axis=1, tiled=True)]
    all_to_all x1, waiting for transfers between devices: 1.15 us -> 5.13 us  [per_device(): lax.all_to_all(jnp.stack(jnp.split(resid, lax.axis_size('xl'), axis=2)),...]
    sub x1, other arithmetic: 4.44 us -> 0.81 us  [per_device(): resid = shift_obs - modelled[None]]
    while x2 -> x0, local copies, waits for them, and re-layouts: 3.44 us -> none  [per_device(): lax.fori_loop(1, 2 * LAGS + 1, one_lag, first_lag)]
    all_to_all x1, starting transfers between devices: 6.08 us -> 3.59 us  [per_device(): lax.all_to_all(confidence, 'xl', split_axis=2, concat_axis=1, tiled=True)]
    unnamed x12 -> x14, local copies, waits for them, and re-layouts: 11.3 us -> 8.86 us
    ppermute x1, waiting for transfers between devices: 0.01 us -> 2.22 us  [extended(): lax.ppermute(lax.slice_in_dim(block, 0, width, axis=dim), axis, backward)]
  transfers between devices with their start and end apart: 4 -> 4, of which waited for: 3 -> 3; matrix products, arithmetic and copies ran while one was open for 14% -> 5% of each run, Pallas kernels for 0% -> 0%
where the time goes in v1:
time: 125 us
  other arithmetic  58.7 us (47%)
  local copies, waits for them, and re-layouts  18.9 us (15%)
  starting transfers between devices  15.5 us (12%)
  waiting for transfers between devices  14.7 us (12%)
  blocking collectives  10.5 us (8%)
  matrix products  2.73 us (2%)
  loops' own time  2.02 us (2%)
  between operations  1.63 us (1%)
    add x98, other arithmetic, box_time(): previous[:, :, :-length] + previous[:, :, length:]  21.5 us
    add x31, other arithmetic, one_lag(): total_corr + normed * weight_exp  12 us
    psum x1, blocking collectives, per_device(): summed = lax.psum(normal, 'inl')  10.5 us
    add x33, other arithmetic, box_time(): total = piece if total is None else total + piece  9.07 us
    unnamed x14, local copies, waits for them, and re-layouts  8.86 us
    all_to_all x1, waiting for transfers between devices, per_device(): lax.all_to_all(confidence, 'xl', split_axis=2, concat_axis=1, tiled=True)  7.35 us
    slice x33, local copies, waits for them, and re-layouts, box_time(): previous[:, :, :-length] + previous[:, :, length:]  5.94 us
    all_to_all x1, starting transfers between devices, per_device(): lax.all_to_all(jnp.stack(jnp.split(resid, lax.axis_size('xl'), axis=2)),...  5.72 us
  transfers between devices with their start and end apart: 4, of which 3 were waited for; matrix products, arithmetic and copies ran while one was open for 5% of the time, Pallas kernels for 0%

profile of v1, /device:TPU:0, one launch (start us, length us, event | category | flops | bytes accessed | tf_op | source)
XLA Modules:
  0.0 124.6 jit_solution(12045519015552787543)
XLA Ops:
  0.6 1.2 pad_maximum_fusion.2
  1.9 4.9 %collective-permute-start = (f32[2,4,3,1024]{3,2,1,0:T(4,128)S(1)}, f32[2,4,3,1024]{3,2,1,0:T(4,128)S(1)}, u32[]{:S(2)}, u32[]{:S(2)}) collective-permute-start(f32[2,4,3,1024]{3,2,1,0:T(4,128)S(1)} %get-tuple-element.486), channel_id=1, source_target_pairs={{0,1},{1,2},{2,3},{3,4},{4,5},{5,6},{6,7},{8,9},{9,10},{10,11},{11... | collective-permute-start | bytes 294920 | tf_op jit(solution)/shard_map/ppermute | solution.py:22
  6.7 1.3 %collective-permute-start.1 = (f32[2,4,3,1024]{3,2,1,0:T(4,128)S(1)}, f32[2,4,3,1024]{3,2,1,0:T(4,128)S(1)}, u32[]{:S(2)}, u32[]{:S(2)}) collective-permute-start(f32[2,4,3,1024]{3,2,1,0:T(4,128)S(1)} %get-tuple-element.487), channel_id=1, source_target_pairs={{1,0},{2,1},{3,2},{4,3},{5,4},{6,5},{7,6},{9,8},{10,9},{11,10},{12... | collective-permute-start | bytes 294920 | tf_op jit(solution)/shard_map/ppermute | solution.py:25
  8.1 0.7 convert_element_type.72
  8.8 0.8 copy.35
  9.7 0.8 convolution_bitcast_fusion
  11.4 2.2 %collective-permute-done.1 = f32[2,4,3,1024]{3,2,1,0:T(4,128)S(1)} collective-permute-done((f32[2,4,3,1024]{3,2,1,0:T(4,128)S(1)}, f32[2,4,3,1024]{3,2,1,0:T(4,128)S(1)}, u32[]{:S(2)}, u32[]{:S(2)}) %collective-permute-start.1) | collective-permute-done | bytes 98336 | tf_op jit(solution)/shard_map/ppermute | solution.py:25
  18.4 56.6 %while.21 = (s32[]{:T(128)}, f32[4,16,1024]{2,1,0:T(8,128)S(1)}, f32[4,16,1024]{2,1,0:T(8,128)S(1)}, f32[4,16,1024]{2,1,0:T(8,128)S(1)}, f32[]{:T(128)}, /*index...) while((s32[]{:T(128)}, f32[4,16,1024]{2,1,0:T(8,128)S(1)}, ...), condition=%wide.region_1.2_spmd, body=%wide.region_0.1_spmd.sunk | while | flops 2143487 | bytes 11726543 | solution.py:153
  75.0 0.8 broadcast_subtract_fusion
  75.8 0.6 fusion.67
  77.0 0.6 fusion.65
  78.3 0.6 fusion.63
  80.7 5.7 %all-to-all-start.1 = ((f32[8,4,16,128]{3,2,1,0:T(8,128)}), f32[8,4,16,128]{3,2,1,0:T(8,128)S(1)}, u32[]{:S(2)}, u32[]{:S(2)}) async-start(f32[8,4,16,128]{3,2,1,0:T(8,128)} %fusion.60), calls=%async_computation.1 | async-start | bytes 524288 | tf_op jit(solution)/shard_map/all_to_all | solution.py:162
  86.4 0.8 copy.33
  87.2 2.3 %reshape.47 = f32[8,1,8192]{2,1,0:T(1,128)} reshape(f32[1024,4,16]{2,1,0:T(4,128)S(1)} %bitcast.79) | data formatting | bytes 524288
  89.5 5.1 %all-to-all-done.1 = f32[8,4,16,128]{3,2,1,0:T(8,128)S(1)} async-done(((f32[8,4,16,128]{3,2,1,0:T(8,128)}), f32[8,4,16,128]{3,2,1,0:T(8,128)S(1)}, u32[]{:S(2)}, u32[]{:S(2)}) %all-to-all-start.1) | async-done | bytes 262176 | tf_op jit(solution)/shard_map/all_to_all | solution.py:162
  94.6 3.6 %all-to-all-start = ((f32[8,1,8192]{2,1,0:T(1,128)}), f32[8,1,8192]{2,1,0:T(1,128)S(1)}, u32[]{:S(2)}, u32[]{:S(2)}) async-start(f32[8,1,8192]{2,1,0:T(1,128)} %reshape.47), calls=%async_computation | async-start | bytes 524288 | tf_op jit(solution)/shard_map/all_to_all | solution.py:164
  98.9 7.3 %all-to-all-done = f32[8,1,8192]{2,1,0:T(1,128)S(1)} async-done(((f32[8,1,8192]{2,1,0:T(1,128)}), f32[8,1,8192]{2,1,0:T(1,128)S(1)}, u32[]{:S(2)}, u32[]{:S(2)}) %all-to-all-start) | async-done | bytes 262176 | tf_op jit(solution)/shard_map/all_to_all | solution.py:164
  106.8 1.3 %reduce = f32[8,8192]{1,0:T(8,128)S(1)} reduce(f32[8,1,8192]{2,1,0:T(1,128)S(1)} %all-to-all-done, f32[]{:T(128)} %broadcast.174), dimensions={1}, to_apply=%all_to_all.14.reduce_sub_computation | reduce | bytes 524292 | tf_op jit(solution)/shard_map/all_to_all | solution.py:164
  108.1 1.5 %reshape.48 = f32[1024,4,16]{2,1,0:T(4,128)S(1)} reshape(f32[8,8192]{1,0:T(8,128)S(1)} %reduce) | data formatting | bytes 524288
  109.6 0.8 copy.34
  111.1 0.9 convolution_bitcast_fusion.2
  112.0 1.0 convolution_bitcast_fusion.1
  113.1 10.5 %psum.7 = f32[20,4,128]{2,1,0:T(4,128)S(1)} all-reduce(f32[20,4,128]{2,1,0:T(4,128)S(1)} %copy.42), channel_id=1, replica_groups=mesh['inl'=4,'xl'=8] {'inl'}, use_global_device_ids=true, to_apply=%region_3.4 | all-reduce | flops 10240 | bytes 81920 | tf_op jit(solution)/shard_map/psum | solution.py:173
  (289 shorter events, 65.6 us)
Async XLA Ops:
  0.6 13.0 %copy-start.1 = (f32[4,16,1024]{2,1,0:T(8,128)S(1)}, f32[4,16,1024]{2,1,0:T(8,128)}, u32[]{:S(2)}) copy-start(f32[4,16,1024]{2,1,0:T(8,128)} %param.7) | copy-start | bytes 786436
  0.6 13.0 %copy-start = (f32[4,16,1024]{2,1,0:T(8,128)S(1)}, f32[4,16,1024]{2,1,0:T(8,128)}, u32[]{:S(2)}) copy-start(f32[4,16,1024]{2,1,0:T(8,128)} %param.8) | copy-start | bytes 786436
  1.9 9.5 %collective-permute-start = (f32[2,4,3,1024]{3,2,1,0:T(4,128)S(1)}, f32[2,4,3,1024]{3,2,1,0:T(4,128)S(1)}, u32[]{:S(2)}, u32[]{:S(2)}) collective-permute-start(f32[2,4,3,1024]{3,2,1,0:T(4,128)S(1)} %get-tuple-element.486), channel_id=1, source_target_pairs={{0,1},{1,2},{2,3},{3,4},{4,5},{5,6},{6,7},{8,9},{9,10},{10,11},{11... | collective-permute-start | bytes 294920 | tf_op jit(solution)/shard_map/ppermute | solution.py:22
  6.7 6.9 %collective-permute-start.1 = (f32[2,4,3,1024]{3,2,1,0:T(4,128)S(1)}, f32[2,4,3,1024]{3,2,1,0:T(4,128)S(1)}, u32[]{:S(2)}, u32[]{:S(2)}) collective-permute-start(f32[2,4,3,1024]{3,2,1,0:T(4,128)S(1)} %get-tuple-element.487), channel_id=1, source_target_pairs={{1,0},{2,1},{3,2},{4,3},{5,4},{6,5},{7,6},{9,8},{10,9},{11,10},{12... | collective-permute-start | bytes 294920 | tf_op jit(solution)/shard_map/ppermute | solution.py:25
  80.7 13.9 %all-to-all-start.1 = ((f32[8,4,16,128]{3,2,1,0:T(8,128)}), f32[8,4,16,128]{3,2,1,0:T(8,128)S(1)}, u32[]{:S(2)}, u32[]{:S(2)}) async-start(f32[8,4,16,128]{3,2,1,0:T(8,128)} %fusion.60), calls=%async_computation.1 | async-start | bytes 524288 | tf_op jit(solution)/shard_map/all_to_all | solution.py:162
  94.6 11.7 %all-to-all-start = ((f32[8,1,8192]{2,1,0:T(1,128)}), f32[8,1,8192]{2,1,0:T(1,128)S(1)}, u32[]{:S(2)}, u32[]{:S(2)}) async-start(f32[8,1,8192]{2,1,0:T(1,128)} %reshape.47), calls=%async_computation | async-start | bytes 524288 | tf_op jit(solution)/shard_map/all_to_all | solution.py:164
